TPU v7x, 128 devices: a whole 4x4x4 slice. The times are simulated.
128 devices in a mesh: llm: 4 (over x), enc: 32 (over y, z, core).
Axes of the slice: x: 4, y: 4, z: 4, core: 2. Of those that a mesh axis runs over, the one named last changes fastest.
Arguments:
- token_gradient: bfloat16 [256, 128, 8192], P('enc', None, 'llm'), may hold values from -6 to 6
- projection: bfloat16 [1280, 8192], P(None, 'llm'), may hold values from -0.0625 to 0.0625
- clip_length: int32 [512], P('enc'), may hold values from 16 to 32, as said below
- clip_offset: int32 [512], P('enc'), may hold values from 0 to 96, as said below
- clip_home: int32 [512], P('enc'), may hold values from 0 to 511, as said below
- block_input: bfloat16 [512, 32, 1280], P('enc'), may hold values from -6 to 6
- block_output: bfloat16 [512, 32, 1280], P('enc'), may hold values from -6 to 6
- norm_gain: float32 [1280], replicated, may hold values from 0.1 to 1.9
- norm_bias: float32 [1280], replicated, may hold values from -3 to 3
- up_weight: bfloat16 [1280, 5120], P('enc', 'llm'), may hold values from -0.15625 to 0.15625
- up_bias: float32 [5120], P('llm'), may hold values from -3 to 3
- down_weight: bfloat16 [5120, 1280], P('llm', 'enc'), may hold values from -0.078125 to 0.078125
- post_gain: float32 [1280], replicated, may hold values from 0.1 to 1.9
Outputs:
- input_gradient: bfloat16 [512, 32, 1280], P('enc', None, 'llm')
- up_gradient: float32 [1280, 5120], P('enc', 'llm')
- down_gradient: float32 [5120, 1280], P('llm', 'enc')
Inputs may be any that keep to these rules, and one draw needn't show every extreme that they name: `clip_length`: each entry of an aligned block of 16 entries is at most 32, and every block holds one entry equal to 32. Clip k starts in part k % 2 of its sequence, the parts being 64 rows long, and clip_offset + 32 stays within that part. `clip_home`: A permutation of the 512 encoder slots; slot j belongs to encoder index j // 16; the clips of one aligned block of 16 entries go to one encoder index at most 1 times, and some encoder index receives exactly 1 of them.
All inputs are finite; a program needn't handle non-finite values.
Results may differ from a plain program's by a relative error of at most 0.0068.
Values may be sent and summed in bfloat16 or wider, within the bound.
No kernel may reach another device: no remote copies, remote signals or barrier semaphores. Data moves between devices by JAX's collectives and lax.ppermute only.
A program may use at most 128 MiB of HBM per device.

v0:
```python
import jax
import jax.numpy as jnp
from jax import lax
from jax.sharding import PartitionSpec as P

CPS = 2
norm_epsilon = 1e-05


def gelu_parts(pre_act):
    normal_cdf = 0.5 * (1.0 + jax.scipy.special.erf(pre_act * 0.7071067811865476))
    normal_pdf = jnp.exp(-0.5 * pre_act * pre_act) * 0.3989422804014327
    return (pre_act * normal_cdf, normal_cdf + pre_act * normal_pdf)


def norm_stats(values):
    row_mean = jnp.mean(values, axis=-1, keepdims=True)
    centred = values - row_mean
    variance = jnp.mean(centred * centred, axis=-1, keepdims=True)
    inverse = lax.rsqrt(variance + norm_epsilon)
    return (centred * inverse, inverse)


def norm_backward(grad_hat, normed_hat, inverse):
    first_mean = jnp.mean(grad_hat, axis=-1, keepdims=True)
    second_mean = jnp.mean(grad_hat * normed_hat, axis=-1, keepdims=True)
    return inverse * (grad_hat - first_mean - normed_hat * second_mean)


def row_contract(left_rows, right_rows):
    return lax.dot_general(
        left_rows, right_rows, (((0,), (0,)), ((), ())), preferred_element_type=jnp.float32
    )


def own_columns(values, column_start, column_span):
    return lax.dynamic_slice_in_dim(values, column_start, column_span, values.ndim - 1)


def project_terms(clip_blocks, projection):
    clips_here, frames, columns = clip_blocks.shape
    flat_rows = clip_blocks.reshape(clips_here * frames, columns)
    partial_terms = lax.dot_general(
        flat_rows, projection, (((1,), (1,)), ((), ())), preferred_element_type=jnp.float32
    )
    return partial_terms.reshape(clips_here, frames, projection.shape[0])


def project_sum(clip_blocks, projection):
    return lax.psum(project_terms(clip_blocks, projection), "llm")


def deliver(clip_blocks, routing, slot_marks):
    clips_here, frames, columns = clip_blocks.shape
    devices, pair_slots, slot_count = slot_marks.shape
    packed = jnp.einsum(
        "bc,cfw->bfw", routing, clip_blocks, preferred_element_type=jnp.float32
    ).astype(jnp.bfloat16)
    packed = packed.reshape(devices, pair_slots, frames, columns)
    received, marks_in = (
        lax.all_to_all(packed, "enc", split_axis=0, concat_axis=0, tiled=True),
        lax.all_to_all(slot_marks, "enc", split_axis=0, concat_axis=0, tiled=True),
    )
    placed = jnp.einsum("npc,npfw->cfw", marks_in, received, preferred_element_type=jnp.float32)
    return placed.astype(jnp.bfloat16)


def shards(
    token_gradient,
    projection,
    clip_length,
    clip_offset,
    clip_home,
    block_input,
    block_output,
    norm_gain,
    norm_bias,
    up_weight,
    up_bias,
    down_weight,
    post_gain,
):
    devices = lax.axis_size("enc")
    clips_here, frames, model_width = block_input.shape
    pair_slots = max(1, clips_here // devices)
    positions = jnp.arange(frames, dtype=jnp.int32)
    clip_order = jnp.arange(clips_here, dtype=jnp.int32)
    target = clip_home // clips_here
    slot_place = clip_home % clips_here
    earlier = clip_order[None, :] < clip_order[:, None]
    same_target = target[None, :] == target[:, None]
    bucket_rank = jnp.sum((earlier & same_target).astype(jnp.int32), axis=1)
    bucket = target * pair_slots + bucket_rank
    buckets = jnp.arange(devices * pair_slots, dtype=jnp.int32)
    routing = (buckets[:, None] == bucket[None, :]).astype(jnp.bfloat16)
    slot_table = (slot_place[:, None] == clip_order[None, :]).astype(jnp.bfloat16)
    slot_marks = jnp.dot(routing, slot_table, preferred_element_type=jnp.float32).astype(
        jnp.bfloat16
    )
    slot_marks = slot_marks.reshape(devices, pair_slots, clips_here)

    def cut_clip(clip_index, offset, length):
        picked = lax.dynamic_slice(
            token_gradient,
            (clip_index // CPS, offset, jnp.int32(0)),
            (1, frames, token_gradient.shape[2]),
        )[0]
        return jnp.where((positions < length)[:, None], picked, jnp.zeros_like(picked))

    clip_blocks = jax.vmap(cut_clip)(clip_order, clip_offset, clip_length)
    feature_grad = project_sum(deliver(clip_blocks, routing, slot_marks), projection).astype(
        jnp.bfloat16
    )
    row_total = clips_here * frames
    feature_rows = feature_grad.reshape(row_total, model_width).astype(jnp.float32)
    output_hat, output_inverse = norm_stats(
        block_output.reshape(row_total, model_width).astype(jnp.float32)
    )
    post_grad = norm_backward(feature_rows * post_gain, output_hat, output_inverse)
    post_rounded = post_grad.astype(jnp.bfloat16)
    input_hat, input_inverse = norm_stats(
        block_input.reshape(row_total, model_width).astype(jnp.float32)
    )
    normed = (input_hat * norm_gain + norm_bias).astype(jnp.bfloat16)
    up_full, down_full = (
        lax.all_gather(up_weight, "enc", axis=0, tiled=True),
        lax.all_gather(down_weight, "enc", axis=1, tiled=True),
    )
    pre_act = jnp.dot(normed, up_full, preferred_element_type=jnp.float32) + up_bias
    activation, gelu_slope = gelu_parts(pre_act)
    act_rounded = activation.astype(jnp.bfloat16)
    act_grad = lax.dot_general(
        post_rounded, down_full, (((1,), (1,)), ((), ())), preferred_element_type=jnp.float32
    )
    pre_grad = (act_grad * gelu_slope).astype(jnp.bfloat16)
    normed_part = lax.dot_general(
        pre_grad, up_full, (((1,), (1,)), ((), ())), preferred_element_type=jnp.float32
    )
    groups = lax.axis_size("llm")
    share_width = model_width // groups
    share_start = lax.axis_index("llm") * share_width
    normed_grad = lax.psum(normed_part, "llm")
    full_grad = post_grad + norm_backward(normed_grad * norm_gain, input_hat, input_inverse)
    input_rows = own_columns(full_grad, share_start, share_width)
    input_gradient = input_rows.astype(jnp.bfloat16).reshape(clips_here, frames, share_width)
    scale_count = clips_here * devices
    up_gradient = (
        lax.psum_scatter(
            row_contract(
                own_columns(normed, jnp.int32(0), up_weight.shape[0] * lax.axis_size("enc")),
                pre_grad,
            ),
            "enc",
            scatter_dimension=0,
            tiled=True,
        )
        / scale_count
    )
    down_gradient = (
        lax.psum_scatter(
            row_contract(
                own_columns(
                    post_rounded, jnp.int32(0), down_weight.shape[1] * lax.axis_size("enc")
                ),
                act_rounded,
            ),
            "enc",
            scatter_dimension=0,
            tiled=True,
        )
        / scale_count
    ).T
    return (input_gradient, up_gradient, down_gradient)


def solution(mesh):
    return jax.shard_map(
        shards,
        mesh=mesh,
        in_specs=(
            P("enc", None, "llm"),
            P(None, "llm"),
            P("enc"),
            P("enc"),
            P("enc"),
            P("enc", None, None),
            P("enc", None, None),
            P(),
            P(),
            P("enc", "llm"),
            P("llm"),
            P("llm", "enc"),
            P(),
        ),
        out_specs=(P("enc", None, "llm"), P("enc", "llm"), P("llm", "enc")),
        check_vma=False,
    )
```

profile of v0, /device:TPU:0, one launch (start us, length us, event | category | flops | bytes accessed | tf_op | source)
XLA Modules:
  0.0 444.9 jit_solution(10234905339764300413)
XLA Ops:
  7.2 0.7 all-gather.5.cloned.1.call-update
  7.9 0.7 and_select_fusion.1
  9.0 0.7 copy.26
  9.7 8.4 %all-to-all-start = ((bf16[32,1,16]{2,1,0:T(2,128)(2,1)}), bf16[32,1,16]{2,1,0:T(2,128)(2,1)S(1)}, u32[]{:S(2)}, u32[]{:S(2)}) async-start(bf16[32,1,16]{2,1,0:T(2,128)(2,1)} %copy.26), calls=%async_computation | async-start | bytes 32768 | tf_op jit(solution)/shard_map/all_to_all | solution.py:62
  18.2 6.5 %copy.28 = bf16[8,128,2048]{2,0,1:T(8,128)(2,1)} copy(bf16[8,128,2048]{2,1,0:T(8,128)(2,1)} %param.13) | data formatting | bytes 8388608 | tf_op args[0]
  24.7 5.8 %gather_fusion = bf16[16,32,2048]{2,0,1:T(8,128)(2,1)S(1)} fusion(bf16[8,128,2048]{2,0,1:T(8,128)(2,1)} %copy.28, s32[16]{0:T(128)S(1)} %fusion.41), kind=kCustom, calls=%fused_computation | custom fusion | bytes 4194496 | tf_op jit(solution)/shard_map/vmap()/gather | solution.py:103
  30.5 1.4 convert_bitcast_fusion
  31.9 4.3 copy.29
  36.1 7.7 %all-to-all-start.1 = ((bf16[32,1,32,2048]{3,2,1,0:T(8,128)(2,1)}), bf16[32,1,32,2048]{3,2,1,0:T(8,128)(2,1)}, u32[]{:S(2)}, u32[]{:S(2)}) async-start(bf16[32,1,32,2048]{3,2,1,0:T(8,128)(2,1)} %copy.29), calls=%async_computation.1 | async-start | bytes 8388608 | tf_op jit(solution)/shard_map/all_to_all | solution.py:61
  43.9 0.7 all-gather.3.cloned.1.call-update
  45.2 0.5 multiply_reduce_fusion.3
  46.1 0.5 multiply_reduce_fusion.1
  46.7 1.9 fusion.13
  48.6 49.8 %all-to-all-done.1 = bf16[32,1,32,2048]{3,2,1,0:T(8,128)(2,1)} async-done(((bf16[32,1,32,2048]{3,2,1,0:T(8,128)(2,1)}), bf16[32,1,32,2048]{3,2,1,0:T(8,128)(2,1)}, u32[]{:S(2)}, u32[]{:S(2)}) %all-to-all-start.1) | async-done | bytes 4194336 | tf_op jit(solution)/shard_map/all_to_all | solution.py:61
  98.4 6.8 %fusion.5 = bf16[16,32,2048]{2,0,1:T(8,128)(2,1)S(1)} fusion(bf16[32,1,32,2048]{3,2,1,0:T(8,128)(2,1)} %all-to-all-done.1, bf16[32,1,16]{0,2,1:T(8,128)(2,1)S(1)} %copy.27), kind=kOutput, calls=%fused_computation.10 | convolution fusion | flops 68157440 | bytes 6292480 | tf_op jit(solution)/shard_map/npc,npfw->cfw/dot_general | solution.py:64
  105.2 8.2 %fusion = f32[16,32,1280]{2,1,0:T(8,128)} fusion(bf16[1280,2048]{1,0:T(8,128)(2,1)} %param.14, bf16[16,32,2048]{2,0,1:T(8,128)(2,1)S(1)} %fusion.5), kind=kOutput, calls=%fused_computation.1 | convolution fusion | flops 2684354560 | bytes 9961472 | tf_op jit(solution)/shard_map/dot_general | solution.py:43
  113.4 54.4 %all-reduce.4 = bf16[16,32,1280]{2,1,0:T(8,128)(2,1)} all-reduce(f32[16,32,1280]{2,1,0:T(8,128)} %fusion), channel_id=1, replica_groups=mesh['llm'=4,'enc'=32] {'llm'}, use_global_device_ids=true, to_apply=%region_3.4 | all-reduce | flops 655360 | bytes 3932160 | tf_op jit(solution)/shard_map/psum | solution.py:50
  167.9 2.1 multiply_reduce_fusion.4
  170.2 3.7 fusion.17
  173.9 6.1 %convolution_add_fusion = f32[512,1280]{1,0:T(8,128)} fusion(bf16[1280,1280]{1,0:T(8,128)(2,1)} %all-gather.5.cloned.1.call-done, f32[1280]{0:T(1024)S(1)} %copy-done.6, f32[512,1280]{1,0:T(8,128)} %fusion.13, f32[1280]{0:T(1024)S(1)} %copy-done.7, f32[1280]{0:T(1024)S(1)} %copy-done.3), kind=kOutput, calls=%fused_computation.9 | convolution fusion | flops 1680343040 | bytes 8535040 | tf_op jit(solution)/shard_map/dot_general | solution.py:129
  180.0 5.9 %fusion.8 = bf16[512,1280]{1,0:T(8,128)(2,1)S(1)} fusion(bf16[1280,1280]{0,1:T(8,128)(2,1)} %all-gather.3.cloned.1.call-done, f32[512,1280]{1,0:T(8,128)} %convolution_add_fusion, f32[512,1280]{1,0:T(8,128)} %fusion.17), kind=kOutput, calls=%fused_computation.11 | convolution fusion | flops 1684930560 | bytes 9830400 | tf_op jit(solution)/shard_map/dot_general | solution.py:132
  185.9 3.4 fusion.47
  189.4 6.4 %fusion.30 = f32[1280,1280]{1,0:T(8,128)} fusion(bf16[512,1280]{1,0:T(8,128)(2,1)S(1)} %fusion.8, f32[512,1280]{1,0:T(8,128)} %fusion.13, f32[1280]{0:T(1024)S(1)} %copy-done.7, f32[1280]{0:T(1024)S(1)} %copy-done.3), kind=kOutput, calls=%fused_computation.51 | convolution fusion | flops 1679687680 | bytes 10496000 | tf_op jit(solution)/shard_map/dot_general | solution.py:31
  195.9 0.3 reduce-scatter.5.cloned.1.call-start
  196.2 7.6 %fusion.22 = f32[1280,1280]{1,0:T(8,128)} fusion(f32[512,1280]{1,0:T(8,128)} %convolution_add_fusion, f32[512,1280]{1,0:T(8,128)} %fusion.17), kind=kOutput, calls=%fused_computation.37 | convolution fusion | flops 1681653760 | bytes 11796480 | tf_op jit(solution)/shard_map/dot_general | solution.py:31
  203.9 53.1 %all-reduce.3.cloned.1.call-done = f32[512,1280]{1,0:T(8,128)} async-done(((f32[512,1280]{1,0:T(8,128)}), f32[512,1280]{1,0:T(8,128)}) %all-reduce.3.cloned.1.call-update) | async-done | bytes 2621456 | tf_op jit(solution)/shard_map/psum | solution.py:142
  257.0 2.6 fusion.46
  259.6 3.3 fusion.25
  262.9 84.2 %reduce-scatter.3.cloned.1.call-done = f32[40,1280]{1,0:T(8,128)} async-done(((f32[1280,1280]{1,0:T(8,128)}), f32[40,1280]{1,0:T(8,128)}) %reduce-scatter.3.cloned.1.call-update) | async-done | bytes 204816 | tf_op jit(solution)/shard_map/reduce_scatter | solution.py:148
  347.2 1.6 broadcast_multiply_fusion.1
  348.8 87.9 %reduce-scatter.5.cloned.1.call-done = f32[40,1280]{1,0:T(8,128)} async-done(((f32[1280,1280]{1,0:T(8,128)}), f32[40,1280]{1,0:T(8,128)}) %reduce-scatter.5.cloned.1.call-update) | async-done | bytes 204816 | tf_op jit(solution)/shard_map/reduce_scatter | solution.py:160
  436.7 1.6 multiply_bitcast_fusion
  (49 shorter events, 2.0 us)
Async XLA Ops:
  7.2 166.7 %all-gather.5.cloned.1.call-start = ((), (), s32[]{:S(2)}) async-start(), calls=%async_computation.5 | async-start | bytes 3379200 | tf_op jit(solution)/shard_map/all_gather | solution.py:126
  9.7 26.4 %all-to-all-start = ((bf16[32,1,16]{2,1,0:T(2,128)(2,1)}), bf16[32,1,16]{2,1,0:T(2,128)(2,1)S(1)}, u32[]{:S(2)}, u32[]{:S(2)}) async-start(bf16[32,1,16]{2,1,0:T(2,128)(2,1)} %copy.26), calls=%async_computation | async-start | bytes 32768 | tf_op jit(solution)/shard_map/all_to_all | solution.py:62
  18.2 6.5 %copy-start.8 = (s32[16]{0:T(128)S(1)}, s32[16]{0:T(128)}, u32[]{:S(2)}) copy-start(s32[16]{0:T(128)} %param.16) | copy-start | bytes 196
  24.7 5.8 %copy-start.4 = (s32[16]{0:T(128)S(1)}, s32[16]{0:T(128)}, u32[]{:S(2)}) copy-start(s32[16]{0:T(128)} %param.15) | copy-start | bytes 196
  36.1 8.7 %copy-start = (bf16[16,32,1280]{2,1,0:T(8,128)(2,1)S(1)}, bf16[16,32,1280]{2,1,0:T(8,128)(2,1)}, u32[]{:S(2)}) copy-start(bf16[16,32,1280]{2,1,0:T(8,128)(2,1)} %param.19) | copy-start | bytes 3932164
  36.1 62.3 %all-to-all-start.1 = ((bf16[32,1,32,2048]{3,2,1,0:T(8,128)(2,1)}), bf16[32,1,32,2048]{3,2,1,0:T(8,128)(2,1)}, u32[]{:S(2)}, u32[]{:S(2)}) async-start(bf16[32,1,32,2048]{3,2,1,0:T(8,128)(2,1)} %copy.29), calls=%async_computation.1 | async-start | bytes 8388608 | tf_op jit(solution)/shard_map/all_to_all | solution.py:61
  43.9 1.9 copy-start.1
  43.9 136.1 %all-gather.3.cloned.1.call-start = ((), (), s32[]{:S(2)}) async-start(), calls=%async_computation.4 | async-start | bytes 3379200 | tf_op jit(solution)/shard_map/all_gather | solution.py:127
  44.6 212.4 %all-reduce.3.cloned.1.call-start = ((), (), s32[]{:S(2)}) async-start(), calls=%async_computation.6 | async-start | bytes 5242880 | tf_op jit(solution)/shard_map/psum | solution.py:142
  113.4 54.4 %copy-start.2 = (f32[1280]{0:T(1024)S(1)}, f32[1280]{0:T(1024)}, u32[]{:S(2)}) copy-start(f32[1280]{0:T(1024)} %param.25) | copy-start | bytes 15364
  170.1 3.7 copy-start.3
  170.1 3.7 copy-start.6
  170.2 3.7 copy-start.7
  180.0 5.9 %copy-start.5 = (bf16[1280,1280]{1,0:T(8,128)(2,1)S(1)}, bf16[1280,1280]{1,0:T(8,128)(2,1)}, u32[]{:S(2)}) copy-start(bf16[1280,1280]{1,0:T(8,128)(2,1)} %all-gather.5.cloned.1.call-done) | copy-start | bytes 9830404
  189.4 157.8 %reduce-scatter.3.cloned.1.call-start = ((), (), s32[]{:S(2)}) async-start(), calls=%async_computation.7 | async-start | bytes 6758400 | tf_op jit(solution)/shard_map/reduce_scatter | solution.py:148
  195.9 240.8 %reduce-scatter.5.cloned.1.call-start = ((), (), s32[]{:S(2)}) async-start(), calls=%async_computation.8 | async-start | bytes 6758400 | tf_op jit(solution)/shard_map/reduce_scatter | solution.py:160
Sparse Core Ops, SparseCore 0:
  10.3 74.7 all-gather.4
  87.5 55.1 all-gather.2
  189.5 67.4 all-reduce.2
  260.6 86.5 reduce-scatter.2
  350.8 85.8 reduce-scatter.4
where the time goes:
time: 445 us
  waiting for transfers between devices  276 us (62%)
  blocking collectives  54.4 us (12%)
  matrix products  46.2 us (10%)
  other arithmetic  19.2 us (4%)
  local copies, waits for them, and re-layouts  17.8 us (4%)
  starting transfers between devices  16.8 us (4%)
  between operations  13.9 us (3%)
    reduce_scatter x1, waiting for transfers between devices, shards(): lax.psum_scatter(row_contract(own_columns(post_rounded, jnp.int32(0), dow...  87.9 us
    reduce_scatter x1, waiting for transfers between devices, shards(): lax.psum_scatter(row_contract(own_columns(normed, jnp.int32(0), up_weight...  84.2 us
    psum x1, blocking collectives, project_sum(): return lax.psum(project_terms(clip_blocks, projection), 'llm')  54.4 us
    psum x1, waiting for transfers between devices, shards(): normed_grad = lax.psum(normed_part, 'llm')  53.1 us
    all_to_all x1, waiting for transfers between devices, deliver(): lax.all_to_all(packed, 'enc', split_axis=0, concat_axis=0, tiled=True)  49.8 us
    dot_general x2, matrix products, row_contract(): lax.dot_general(left_rows, right_rows, (((0,), (0,)), ((), ())), preferre...  14.1 us
  transfers between devices with their start and end apart: 7, of which 4 were waited for; matrix products, arithmetic and copies ran while one was open for 16% of the time, Pallas kernels for 0%

commit v1 on v0

--- a/solution.py
+++ b/solution.py
@@ -47,7 +47,7 @@
 
 
 def project_sum(clip_blocks, projection):
-    return lax.psum(project_terms(clip_blocks, projection), "llm")
+    return jnp.sum(lax.all_gather(project_terms(clip_blocks, projection), "llm"), axis=0)
 
 
 def deliver(clip_blocks, routing, slot_marks):

time: 445 us -> 531 us (1.19)
  waiting for transfers between devices: 276 us -> 409 us
  blocking collectives: 54.4 us -> 0 us
  other arithmetic: 19.2 us -> 25.5 us
    all_gather x0 -> x1, waiting for transfers between devices: none -> 93.2 us  [project_sum(): lax.all_gather(project_terms(clip_blocks, projection), 'llm')]
    psum x1 -> x0, blocking collectives: 54.4 us -> none  [project_sum(): return lax.psum(project_terms(clip_blocks, projection), 'llm')]
    all_gather x1, waiting for transfers between devices: 0.01 us -> 36.2 us  [shards(): lax.all_gather(down_weight, 'enc', axis=1, tiled=True)]
    reduce_sum x0 -> x1, other arithmetic: none -> 6.3 us  [project_sum(): jnp.sum(lax.all_gather(project_terms(clip_blocks, projection), 'llm'), ax...]
  transfers between devices with their start and end apart: 7 -> 8, of which waited for: 4 -> 6; matrix products, arithmetic and copies ran while one was open for 16% -> 15% of each run, Pallas kernels for 0% -> 0%
where the time goes in v1:
time: 531 us; the launch traced here: 530 us
  waiting for transfers between devices  409 us (77%)
  matrix products  46.1 us (9%)
  other arithmetic  25.5 us (5%)
  local copies, waits for them, and re-layouts  18.2 us (3%)
  starting transfers between devices  16.9 us (3%)
  between operations  14.2 us (3%)
    all_gather x1, waiting for transfers between devices, project_sum(): lax.all_gather(project_terms(clip_blocks, projection), 'llm')  93.2 us
    reduce_scatter x1, waiting for transfers between devices, shards(): lax.psum_scatter(row_contract(own_columns(post_rounded, jnp.int32(0), dow...  88 us
    reduce_scatter x1, waiting for transfers between devices, shards(): lax.psum_scatter(row_contract(own_columns(normed, jnp.int32(0), up_weight...  84.2 us
    all_to_all x1, waiting for transfers between devices, deliver(): lax.all_to_all(packed, 'enc', split_axis=0, concat_axis=0, tiled=True)  54.3 us
    psum x1, waiting for transfers between devices, shards(): normed_grad = lax.psum(normed_part, 'llm')  52.1 us
    all_gather x1, waiting for transfers between devices, shards(): lax.all_gather(down_weight, 'enc', axis=1, tiled=True)  36.2 us
    dot_general x2, matrix products, row_contract(): lax.dot_general(left_rows, right_rows, (((0,), (0,)), ((), ())), preferre...  14 us
  transfers between devices with their start and end apart: 8, of which 6 were waited for; matrix products, arithmetic and copies ran while one was open for 15% of the time, Pallas kernels for 0%

profile of v1, /device:TPU:0, one launch (start us, length us, event | category | flops | bytes accessed | tf_op | source)
XLA Modules:
  0.0 530.4 jit_solution(16177098980703635062)
XLA Ops:
  7.2 0.7 all-gather.7.cloned.1.call-update
  7.9 0.7 and_select_fusion.1
  9.0 0.7 copy.26
  9.7 8.4 %all-to-all-start = ((bf16[32,1,16]{2,1,0:T(2,128)(2,1)}), bf16[32,1,16]{2,1,0:T(2,128)(2,1)S(1)}, u32[]{:S(2)}, u32[]{:S(2)}) async-start(bf16[32,1,16]{2,1,0:T(2,128)(2,1)} %copy.26), calls=%async_computation | async-start | bytes 32768 | tf_op jit(solution)/shard_map/all_to_all | solution.py:62
  18.2 6.5 %copy.28 = bf16[8,128,2048]{2,0,1:T(8,128)(2,1)} copy(bf16[8,128,2048]{2,1,0:T(8,128)(2,1)} %param.13) | data formatting | bytes 8388608 | tf_op args[0]
  24.7 5.8 %gather_fusion = bf16[16,32,2048]{2,0,1:T(8,128)(2,1)S(1)} fusion(bf16[8,128,2048]{2,0,1:T(8,128)(2,1)} %copy.28, s32[16]{0:T(128)S(1)} %fusion.41), kind=kCustom, calls=%fused_computation | custom fusion | bytes 4194496 | tf_op jit(solution)/shard_map/vmap()/gather | solution.py:103
  30.5 1.3 convert_bitcast_fusion
  31.8 4.4 copy.29
  36.2 7.6 %all-to-all-start.1 = ((bf16[32,1,32,2048]{3,2,1,0:T(8,128)(2,1)}), bf16[32,1,32,2048]{3,2,1,0:T(8,128)(2,1)}, u32[]{:S(2)}, u32[]{:S(2)}) async-start(bf16[32,1,32,2048]{3,2,1,0:T(8,128)(2,1)} %copy.29), calls=%async_computation.1 | async-start | bytes 8388608 | tf_op jit(solution)/shard_map/all_to_all | solution.py:61
  44.1 54.3 %all-to-all-done.1 = bf16[32,1,32,2048]{3,2,1,0:T(8,128)(2,1)} async-done(((bf16[32,1,32,2048]{3,2,1,0:T(8,128)(2,1)}), bf16[32,1,32,2048]{3,2,1,0:T(8,128)(2,1)}, u32[]{:S(2)}, u32[]{:S(2)}) %all-to-all-start.1) | async-done | bytes 4194336 | tf_op jit(solution)/shard_map/all_to_all | solution.py:61
  98.4 6.8 %fusion.5 = bf16[16,32,2048]{2,0,1:T(8,128)(2,1)S(1)} fusion(bf16[32,1,32,2048]{3,2,1,0:T(8,128)(2,1)} %all-to-all-done.1, bf16[32,1,16]{0,2,1:T(8,128)(2,1)S(1)} %copy.27), kind=kOutput, calls=%fused_computation.10 | convolution fusion | flops 68157440 | bytes 6292480 | tf_op jit(solution)/shard_map/npc,npfw->cfw/dot_general | solution.py:64
  105.2 8.2 %fusion = f32[16,32,1280]{2,1,0:T(8,128)} fusion(bf16[1280,2048]{1,0:T(8,128)(2,1)} %param.14, bf16[16,32,2048]{2,0,1:T(8,128)(2,1)S(1)} %fusion.5), kind=kOutput, calls=%fused_computation.1 | convolution fusion | flops 2684354560 | bytes 9961472 | tf_op jit(solution)/shard_map/dot_general | solution.py:43
  113.5 0.7 all-gather.5.cloned.1.call-update
  116.0 0.5 multiply_reduce_fusion.1
  116.6 1.9 fusion.13
  118.5 6.2 %convolution_add_fusion = f32[512,1280]{1,0:T(8,128)} fusion(bf16[1280,1280]{1,0:T(8,128)(2,1)} %all-gather.7.cloned.1.call-done, f32[1280]{0:T(1024)S(1)} %copy-done.6, f32[512,1280]{1,0:T(8,128)} %fusion.13, f32[1280]{0:T(1024)S(1)} %copy-done.7, f32[1280]{0:T(1024)S(1)} %copy-done.3), kind=kOutput, calls=%fused_computation.9 | convolution fusion | flops 1680343040 | bytes 8535040 | tf_op jit(solution)/shard_map/dot_general | solution.py:129
  124.6 93.2 %all-gather.9.cloned.1.call-done = f32[64,32,1280]{2,1,0:T(8,128)} async-done(((f32[16,32,1280]{2,1,0:T(8,128)}), f32[64,32,1280]{2,1,0:T(8,128)}) %all-gather.9.cloned.1.call-update) | async-done | bytes 10485776 | tf_op jit(solution)/shard_map/all_gather | solution.py:50
  217.8 6.3 %reduce_sum.93 = bf16[16,32,1280]{2,1,0:T(8,128)(2,1)} reduce(f32[4,16,32,1280]{3,2,1,0:T(8,128)} %bitcast.56, f32[]{:T(128)} %constant.66.clone.1), dimensions={0}, to_apply=%region_3.4 | reduce | flops 1966080 | bytes 11796484 | tf_op jit(solution)/shard_map/reduce_sum | solution.py:50
  224.1 2.1 multiply_reduce_fusion.4
  226.4 3.7 fusion.17
  230.1 36.2 %all-gather.5.cloned.1.call-done = bf16[1280,1280]{0,1:T(8,128)(2,1)} async-done(((bf16[1280,40]{0,1:T(8,128)(2,1)}), bf16[1280,1280]{0,1:T(8,128)(2,1)}) %all-gather.5.cloned.1.call-update) | async-done | bytes 3276816 | tf_op jit(solution)/shard_map/all_gather | solution.py:127
  266.3 5.9 %fusion.8 = bf16[512,1280]{1,0:T(8,128)(2,1)S(1)} fusion(bf16[1280,1280]{0,1:T(8,128)(2,1)} %all-gather.5.cloned.1.call-done, f32[512,1280]{1,0:T(8,128)} %convolution_add_fusion, f32[512,1280]{1,0:T(8,128)} %fusion.17), kind=kOutput, calls=%fused_computation.11 | convolution fusion | flops 1684930560 | bytes 9830400 | tf_op jit(solution)/shard_map/dot_general | solution.py:132
  272.2 3.4 fusion.47
  275.7 6.4 %fusion.30 = f32[1280,1280]{1,0:T(8,128)} fusion(bf16[512,1280]{1,0:T(8,128)(2,1)S(1)} %fusion.8, f32[512,1280]{1,0:T(8,128)} %fusion.13, f32[1280]{0:T(1024)S(1)} %copy-done.7, f32[1280]{0:T(1024)S(1)} %copy-done.3), kind=kOutput, calls=%fused_computation.51 | convolution fusion | flops 1679687680 | bytes 10496000 | tf_op jit(solution)/shard_map/dot_general | solution.py:31
  282.4 7.6 %fusion.22 = f32[1280,1280]{1,0:T(8,128)} fusion(f32[512,1280]{1,0:T(8,128)} %convolution_add_fusion, f32[512,1280]{1,0:T(8,128)} %fusion.17), kind=kOutput, calls=%fused_computation.37 | convolution fusion | flops 1681653760 | bytes 11796480 | tf_op jit(solution)/shard_map/dot_general | solution.py:31
  290.1 52.1 %all-reduce.2.cloned.1.call-done = f32[512,1280]{1,0:T(8,128)} async-done(((f32[512,1280]{1,0:T(8,128)}), f32[512,1280]{1,0:T(8,128)}) %all-reduce.2.cloned.1.call-update) | async-done | bytes 2621456 | tf_op jit(solution)/shard_map/psum | solution.py:142
  342.2 2.6 fusion.46
  344.8 3.3 fusion.25
  348.1 84.2 %reduce-scatter.3.cloned.1.call-done = f32[40,1280]{1,0:T(8,128)} async-done(((f32[1280,1280]{1,0:T(8,128)}), f32[40,1280]{1,0:T(8,128)}) %reduce-scatter.3.cloned.1.call-update) | async-done | bytes 204816 | tf_op jit(solution)/shard_map/reduce_scatter | solution.py:148
  432.4 1.6 broadcast_multiply_fusion.1
  434.0 88.0 %reduce-scatter.5.cloned.1.call-done = f32[40,1280]{1,0:T(8,128)} async-done(((f32[1280,1280]{1,0:T(8,128)}), f32[40,1280]{1,0:T(8,128)}) %reduce-scatter.5.cloned.1.call-update) | async-done | bytes 204816 | tf_op jit(solution)/shard_map/reduce_scatter | solution.py:160
  521.9 1.6 multiply_bitcast_fusion
  (52 shorter events, 3.3 us)
Async XLA Ops:
  7.2 111.3 %all-gather.7.cloned.1.call-start = ((), (), s32[]{:S(2)}) async-start(), calls=%async_computation.5 | async-start | bytes 3379200 | tf_op jit(solution)/shard_map/all_gather | solution.py:126
  9.7 26.5 %all-to-all-start = ((bf16[32,1,16]{2,1,0:T(2,128)(2,1)}), bf16[32,1,16]{2,1,0:T(2,128)(2,1)S(1)}, u32[]{:S(2)}, u32[]{:S(2)}) async-start(bf16[32,1,16]{2,1,0:T(2,128)(2,1)} %copy.26), calls=%async_computation | async-start | bytes 32768 | tf_op jit(solution)/shard_map/all_to_all | solution.py:62
  18.2 6.5 %copy-start.8 = (s32[16]{0:T(128)S(1)}, s32[16]{0:T(128)}, u32[]{:S(2)}) copy-start(s32[16]{0:T(128)} %param.16) | copy-start | bytes 196
  24.7 5.8 %copy-start.4 = (s32[16]{0:T(128)S(1)}, s32[16]{0:T(128)}, u32[]{:S(2)}) copy-start(s32[16]{0:T(128)} %param.15) | copy-start | bytes 196
  36.2 62.2 %all-to-all-start.1 = ((bf16[32,1,32,2048]{3,2,1,0:T(8,128)(2,1)}), bf16[32,1,32,2048]{3,2,1,0:T(8,128)(2,1)}, u32[]{:S(2)}, u32[]{:S(2)}) async-start(bf16[32,1,32,2048]{3,2,1,0:T(8,128)(2,1)} %copy.29), calls=%async_computation.1 | async-start | bytes 8388608 | tf_op jit(solution)/shard_map/all_to_all | solution.py:61
  43.8 174.0 %all-gather.9.cloned.1.call-start = ((), (), s32[]{:S(2)}) async-start(), calls=%async_computation.9 | async-start | bytes 13107200 | tf_op jit(solution)/shard_map/all_gather | solution.py:50
  113.4 1.3 copy-start
  113.4 2.2 copy-start.1
  113.4 152.8 %all-gather.5.cloned.1.call-start = ((), (), s32[]{:S(2)}) async-start(), calls=%async_computation.4 | async-start | bytes 3379200 | tf_op jit(solution)/shard_map/all_gather | solution.py:127
  114.2 228.0 %all-reduce.2.cloned.1.call-start = ((), (), s32[]{:S(2)}) async-start(), calls=%async_computation.6 | async-start | bytes 5242880 | tf_op jit(solution)/shard_map/psum | solution.py:142
  116.0 2.5 copy-start.3
  116.0 2.5 copy-start.6
  116.0 2.5 copy-start.7
  217.8 6.3 %copy-start.2 = (f32[1280]{0:T(1024)S(1)}, f32[1280]{0:T(1024)}, u32[]{:S(2)}) copy-start(f32[1280]{0:T(1024)} %param.25) | copy-start | bytes 15364
  266.3 5.9 %copy-start.5 = (bf16[1280,1280]{1,0:T(8,128)(2,1)S(1)}, bf16[1280,1280]{1,0:T(8,128)(2,1)}, u32[]{:S(2)}) copy-start(bf16[1280,1280]{1,0:T(8,128)(2,1)} %all-gather.7.cloned.1.call-done) | copy-start | bytes 9830404
  275.7 156.7 %reduce-scatter.3.cloned.1.call-start = ((), (), s32[]{:S(2)}) async-start(), calls=%async_computation.7 | async-start | bytes 6758400 | tf_op jit(solution)/shard_map/reduce_scatter | solution.py:148
  282.1 239.8 %reduce-scatter.5.cloned.1.call-start = ((), (), s32[]{:S(2)}) async-start(), calls=%async_computation.8 | async-start | bytes 6758400 | tf_op jit(solution)/shard_map/reduce_scatter | solution.py:160
Sparse Core Ops, SparseCore 0:
  10.3 74.9 all-gather.6
  113.6 104.1 all-gather.8
  220.1 46.1 all-gather.4
  275.8 66.3 all-reduce.1
  345.8 86.5 reduce-scatter.2
  436.0 85.9 reduce-scatter.4
